TPU v7x, 512 devices: a whole 4x4x16 slice. The times are simulated.
512 devices in a mesh: aux: 32 (over z, y_hi), pair: 16 (over x, y_lo, core).
Axes of the slice: x: 4, y: 4 (y_hi: 2, y_lo: 2; y = y_hi * 2 + y_lo), z: 16, core: 2. Of those that a mesh axis runs over, the one named last changes fastest.
Arguments:
- integrals: float32 [2048, 16, 320], P('aux', 'pair'), may hold values from -0.6 to 0.6
- metric_root: float32 [2048, 2048], P('aux'), as said below
- occ_energy: float32 [16], replicated, may hold values from -2 to -0.3
- virt_energy: float32 [320], replicated, may hold values from 0.3 to 3
- partner: int32 [1, 16], replicated, may hold values from 0 to 15, as said below
Outputs:
- density: float32 [2048, 16, 320], P('aux', 'pair')
Inputs may be any that keep to these rules, and one draw needn't show every extreme that they name: For each r there is one m_r in 1 .. 15 with partner[r, I] = I XOR m_r for every block I; the m_r of different rows differ, so each row is a perfect matching of the blocks. metric_root is symmetric.
All inputs are finite; a program needn't handle non-finite values.
Results may differ from a plain program's by a relative error of at most 0.0003.
Values sent between devices are 32-bit elements; how exact they have to be, the bound alone decides.
A program may use at most 64 MiB of HBM per device.

v0:
```python
from functools import partial

import jax
import jax.numpy as jnp
from jax import lax
from jax.sharding import PartitionSpec as P

highest = lax.Precision.HIGHEST


def partner_2(value, axis, apart):
    mask = 2**apart
    pairs = [(source, source ^ mask) for source in range(lax.axis_size(axis))]
    return lax.ppermute(value, axis, pairs)


def combine_amplitudes(summed, own_energy, partner_energy, virt_energy):
    occ_count = own_energy.shape[0]
    vir_count = virt_energy.shape[0]
    occ_pair = own_energy[:, None] + partner_energy[None, :]
    denominator = (
        occ_pair[:, None, :, None]
        - virt_energy[None, :, None, None]
        - virt_energy[None, None, None, :]
    )
    amplitudes = summed.reshape(occ_count, vir_count, occ_count, vir_count) / denominator
    combined = 2.0 * amplitudes - jnp.transpose(amplitudes, (0, 3, 2, 1))
    return combined.reshape(occ_count * vir_count, occ_count * vir_count)


def fixed_mask(mask_value, bit_count, own_rows):
    current = own_rows
    for bit_id in range(bit_count):
        if mask_value >> bit_id & 1:
            current = partner_2(current, "pair", bit_id)
    return current


def partial_pair(own_rows, partner_rows):
    return lax.dot_general(
        own_rows,
        partner_rows,
        (((0,), (0,)), ((), ())),
        precision=highest,
        preferred_element_type=jnp.float32,
    )


def sum_round(partial_term):
    return lax.psum(partial_term, "aux")


def shards(integrals, metric_root, occ_energy, virt_energy, partner):
    aux_dev, occ_count, vir_count = integrals.shape
    row_width = occ_count * vir_count
    flat_rows = integrals.reshape(aux_dev, row_width)
    factors = jnp.dot(
        metric_root,
        lax.all_gather(flat_rows, "aux", axis=0, tiled=True),
        preferred_element_type=jnp.float32,
        precision=highest,
    )
    own_block = lax.axis_index("pair")
    xor_masks = [partner[0, 0]]
    other_ids = [jnp.bitwise_xor(own_block, xor_mask) for xor_mask in xor_masks]
    bit_count = lax.axis_size("pair").bit_length() - 1
    branches = [
        partial(fixed_mask, mask_value, bit_count) for mask_value in range(1, lax.axis_size("pair"))
    ]
    partner_blocks = [lax.switch(xor_mask - 1, branches, factors) for xor_mask in xor_masks]
    all_rows = [factors] + partner_blocks
    all_ids = [own_block] + other_ids
    partials = [partial_pair(factors, partner_rows) for partner_rows in all_rows]
    summed_list = [sum_round(partial_term) for partial_term in partials]
    own_energy = lax.dynamic_slice_in_dim(occ_energy, own_block * occ_count, occ_count, 0)
    density = jnp.zeros((aux_dev, row_width), jnp.float32)
    for summed, partner_rows, other_id in zip(summed_list, all_rows, all_ids):
        partner_energy = lax.dynamic_slice_in_dim(occ_energy, other_id * occ_count, occ_count, 0)
        combined = combine_amplitudes(summed, own_energy, partner_energy, virt_energy)
        density = density + lax.dot_general(
            partner_rows,
            combined,
            (((1,), (1,)), ((), ())),
            precision=highest,
            preferred_element_type=jnp.float32,
        )
    return density.reshape(aux_dev, occ_count, vir_count)


def solution(mesh):
    in_specs = (P("aux", "pair", None), P("aux", None), P(), P(), P())
    out_specs = P("aux", "pair", None)
    return jax.shard_map(shards, mesh=mesh, in_specs=in_specs, out_specs=out_specs, check_vma=False)
```

profile of v0, /device:TPU:6, one launch (start us, length us, event | category | flops | bytes accessed | tf_op | source)
XLA Modules:
  0.0 514.7 jit_solution(17256896378221130686)
XLA Ops:
  6.5 0.0 copy-start
  6.5 0.0 all-gather.3.cloned.1.call-start
  6.5 0.7 all-gather.3.cloned.1.call-update
  7.3 0.0 all-reduce.3.cloned.1.call-start
  8.0 163.9 %all-gather.3.cloned.1.call-done = f32[2048,1,320]{2,1,0:T(1,128)} async-done(((f32[64,1,320]{2,1,0:T(1,128)}), f32[2048,1,320]{2,1,0:T(1,128)}) %all-gather.3.cloned.1.call-update) | async-done | bytes 2621456 | tf_op jit(solution)/shard_map/all_gather | solution.py:59
  171.9 7.0 %copy.13 = f32[2048,1,320]{0,2,1:T(8,128)S(1)} copy(f32[2048,1,320]{2,1,0:T(1,128)} %all-gather.3.cloned.1.call-done) | data formatting | bytes 5242880 | tf_op jit(solution)/shard_map/all_gather | solution.py:59
  178.9 0.0 copy-done
  178.9 0.0 copy-start.3
  178.9 0.0 copy-start.2
  178.9 0.0 copy-start.1
  178.9 2.4 fusion
  181.3 1.4 fusion.17
  182.7 11.5 %conditional.1 = (f32[64,320]{1,0:T(8,128)}) conditional(s32[]{:T(128)} %clamp.3, f32[64,320]{1,0:T(8,128)S(1)} %fusion, f32[64,320]{1,0:T(8,128)S(1)} %fusion, f32[64,320]{1,0:T(8,128)S(1)} %fusion, f32[64,320]{1,0:T(8,128)S(1)} %fusion, f32[64,320]{1,0:T(8,128)S(1)} %fusion, f32[64,320]{1,0:T(8,128)S(1)} %fusion, ...), branch_computations={%region_1.0_spmd, %region_2.0_spmd, %region_3.0_spmd, %region_4.0_... | conditional | bytes 1310888 | solution.py:70
  182.7 1.9 collective-permute-start.13
  184.6 1.3 collective-permute-done.13
  185.9 3.3 collective-permute-start.14
  189.3 5.0 collective-permute-done.14
  194.3 2.3 fusion.18
  196.6 0.0 all-reduce.3.cloned.1.call-update
  196.6 0.0 copy-done.3
  196.6 0.0 copy-done.2
  196.6 0.6 fusion.16
  199.8 0.0 copy-done.1
  199.8 303.7 %all-reduce.3.cloned.1.call-done = (f32[320,320]{1,0:T(8,128)}, f32[320,320]{1,0:T(8,128)}) async-done(((f32[320,320]{1,0:T(8,128)}, f32[320,320]{1,0:T(8,128)}), (f32[320,320]{1,0:T(8,128)}, f32[320,320]{1,0:T(8,128)})) %all-reduce.3.cloned.1.call-update) | async-done | bytes 819216 | tf_op jit(solution)/shard_map/psum | solution.py:50
  503.5 1.4 subtract_divide_fusion
  504.9 0.2 copy.14
  505.1 0.5 fusion.6
  505.6 0.2 copy.15
  505.8 1.4 fusion.2
  507.1 0.7 copy.16
  (1 shorter events, 0.0 us)
Async XLA Ops:
  6.5 172.3 %copy-start = (f32[64,2048]{1,0:T(8,128)S(1)}, f32[64,2048]{1,0:T(8,128)}, u32[]{:S(2)}) copy-start(f32[64,2048]{1,0:T(8,128)} %param.21) | copy-start | bytes 1572868
  6.5 165.3 %all-gather.3.cloned.1.call-start = ((), (), s32[]{:S(2)}) async-start(), calls=%async_computation | async-start | bytes 3244032 | tf_op jit(solution)/shard_map/all_gather | solution.py:59
  7.3 496.2 %all-reduce.3.cloned.1.call-start = ((), (), s32[]{:S(2)}) async-start(), calls=%async_computation.1 | async-start | bytes 1966080 | tf_op jit(solution)/shard_map/psum | solution.py:50
  178.9 17.7 %copy-start.3 = (s32[1,16]{1,0:T(1,128)S(1)}, s32[1,16]{1,0:T(1,128)}, u32[]{:S(2)}) copy-start(s32[1,16]{1,0:T(1,128)} %param.24) | copy-start | bytes 196
  178.9 17.7 %copy-start.2 = (f32[16]{0:T(128)S(1)}, f32[16]{0:T(128)}, u32[]{:S(2)}) copy-start(f32[16]{0:T(128)} %param.22) | copy-start | bytes 196
  178.9 20.9 %copy-start.1 = (f32[320]{0:T(512)S(1)}, f32[320]{0:T(512)}, u32[]{:S(2)}) copy-start(f32[320]{0:T(512)} %param.23) | copy-start | bytes 3844
  182.7 3.2 collective-permute-start.13
  185.9 8.3 %collective-permute-start.14 = (f32[64,320]{1,0:T(8,128)S(1)}, f32[64,320]{1,0:T(8,128)}, u32[]{:S(2)}, u32[]{:S(2)}) collective-permute-start(f32[64,320]{1,0:T(8,128)S(1)} %collective-permute-done.13), channel_id=1, source_target_pairs={{0,8},{1,9},{2,10},{3,11},{4,12},{5,13},{6,14},{7,15},{8,0},{9,1},... | collective-permute-start | bytes 245768 | tf_op jit(solution)/shard_map/cond/branch_8_fun/ppermute | solution.py:14
Sparse Core Ops, SparseCore 0:
  10.4 161.3 all-gather.2
  196.7 306.7 all-reduce.2
where the time goes:
time: 513 us; the launch traced here: 515 us
  waiting for transfers between devices  475 us (93%)
  between operations  16.7 us (3%)
  local copies, waits for them, and re-layouts  8.82 us (2%)
  matrix products  7.93 us (2%)
  starting transfers between devices  5.29 us (1%)
    psum x1, waiting for transfers between devices, sum_round(): return lax.psum(partial_term, 'aux')  304 us
    all_gather x1, waiting for transfers between devices, shards(): lax.all_gather(flat_rows, 'aux', axis=0, tiled=True)  164 us
  transfers between devices with their start and end apart: 4, of which 4 were waited for; matrix products, arithmetic and copies ran while one was open for 0% of the time, Pallas kernels for 0%

commit v1 on v0

v1 whole, which is shorter than its diff:
```python
import functools

import jax
import jax.numpy as jnp
from jax import lax
from jax.experimental import pallas as pl
from jax.experimental.pallas import tpu as pltpu
from jax.sharding import PartitionSpec as P

MESH = pl.DeviceIdType.MESH
HIGHEST = lax.Precision.HIGHEST


def flip(index, bit):
    return index + bit - 2 * bit * ((index // bit) % 2)


def dot(left, right, dims):
    return lax.dot_general(
        left, right, (dims, ((), ())), precision=HIGHEST, preferred_element_type=jnp.float32
    )


def kernel(
    nz, bits, cut,
    partner_ref, occ_ref, ints_ref, metric_ref, vrow_ref, vcol_ref, out_ref,
    gat, fac, fj, bf, sums, den, rneg, rpos, ybuf, full, total,
    y_s, y_r, gs, gr, bs, br, ns, nr, ps, pr, y2_s, y2_r, as_, ar,
):
    aux = lax.axis_index("aux")
    pair = lax.axis_index("pair")
    z = aux // 2
    yh = aux % 2
    rows, vir = ints_ref.shape
    up = lax.rem(z + 1, nz) * 2 + yh
    down = lax.rem(z + nz - 1, nz) * 2 + yh
    across = z * 2 + 1 - yh
    half = nz // 2

    barrier = pltpu.get_barrier_semaphore()
    for other in (up, down, across):
        pl.semaphore_signal(barrier, inc=1, device_id={"aux": other, "pair": pair}, device_id_type=MESH)
    for b in range(bits):
        pl.semaphore_signal(barrier, inc=1, device_id={"aux": aux, "pair": flip(pair, 2**b)}, device_id_type=MESH)
    pl.semaphore_wait(barrier, 3 + bits)

    def remote(src, dst, s, r, dev_aux, dev_pair=None):
        return pltpu.make_async_remote_copy(
            src_ref=src, dst_ref=dst, send_sem=s, recv_sem=r,
            device_id={"aux": dev_aux, "pair": pair if dev_pair is None else dev_pair},
            device_id_type=MESH,
        )

    mine = gat.at[z, yh]
    mine[...] = ints_ref[...]
    ycopy = remote(ints_ref, mine, y_s, y_r, across)
    ycopy.start()

    def ring(step, d, h):
        block = lax.rem(z - step + nz, nz) if d == 0 else lax.rem(z + step, nz)
        part = yh if h == 0 else 1 - yh
        ref = gat.at[block, part]
        src = ints_ref if h == 0 and isinstance(step, int) and step == 0 else ref
        return remote(src, ref, gs.at[d, h, step], gr.at[d, h, step], up if d == 0 else down)

    def arrived(step, d):
        return lax.rem(z - step - 1 + nz, nz) if d == 0 else lax.rem(z + step + 1, nz)

    def accumulate(block):
        columns = pl.ds(pl.multiple_of(block * 2 * rows, 2 * rows), 2 * rows)
        fac[...] += dot(metric_ref[:, columns], gat[block].reshape(2 * rows, vir), ((1,), (0,)))

    for d in range(2):
        ring(0, d, 0).start()
    fac[...] = jnp.zeros_like(fac)
    for which in range(2):
        own = occ_ref[pair]
        e = own + own if which == 0 else own + occ_ref[partner_ref[0, pair]]
        den[pl.ds(which * half, half)] = (e - vcol_ref[...] - vrow_ref[...]).reshape(half, cut, vir)
    ycopy.wait()
    for d in range(2):
        ring(0, d, 1).start()
    accumulate(z)

    def gather_step(step, carry):
        for h in range(2):
            for d in range(2):
                ring(step - 1, d, h).wait_recv()
                if d == 0:
                    ring(step, d, h).start()
                else:
                    @pl.when(step < half - 1)
                    def _():
                        ring(step, d, h).start()
        for d in range(2):
            accumulate(arrived(step - 1, d))
        return carry

    lax.fori_loop(1, half, gather_step, 0)
    for h in range(2):
        ring(half - 1, 0, h).wait_recv()
    accumulate(arrived(half - 1, 0))

    def gather_drain(step, carry):
        for h in range(2):
            ring(step, 0, h).wait_send()

            @pl.when(step < half - 1)
            def _():
                ring(step, 1, h).wait_send()
        return carry

    lax.fori_loop(0, half, gather_drain, 0)

    mask = partner_ref[0, 0]
    bf[0] = fac[...]
    for b in range(bits):
        copy = remote(bf.at[2 * b], bf.at[2 * b + 1], bs.at[b], br.at[b], aux, flip(pair, 2**b))
        copy.start()
        if b == 0:
            sums[pl.ds(0, half)] = dot(fac[...], fac[...], ((0,), (0,))).reshape(half, cut, vir)
        copy.wait()
        bit = (mask // 2**b) % 2
        chosen = jnp.where(bit == 1, bf[2 * b + 1], bf[2 * b])
        if b < bits - 1:
            bf[2 * b + 2] = chosen
        else:
            fj[...] = chosen
    sums[pl.ds(half, half)] = dot(fac[...], fj[...], ((0,), (0,))).reshape(half, cut, vir)

    def down_copy(step):
        src = rneg.at[step]
        return remote(src, rneg.at[step + 1], ns.at[step], nr.at[step], down)

    def up_copy(step):
        return remote(rpos.at[step], rpos.at[step + 1], ps.at[step], pr.at[step], up)

    rneg[0] = sums[lax.rem(z - half + nz, nz)]
    rpos[0] = sums[lax.rem(z + half - 1, nz)]
    down_copy(0).start()
    up_copy(0).start()

    def reduce_step(step, carry):
        down_copy(step - 1).wait_recv()
        rneg[step] += sums[lax.rem(z - half + step + nz, nz)]
        down_copy(step).start()
        up_copy(step - 1).wait_recv()
        rpos[step] += sums[lax.rem(z + half - 1 - step, nz)]

        @pl.when(step < half - 1)
        def _():
            up_copy(step).start()
        return carry

    lax.fori_loop(1, half, reduce_step, 0)
    down_copy(half - 1).wait_recv()
    total[...] = rneg[half] + rpos[half - 1]
    y2 = remote(total, ybuf, y2_s, y2_r, across)
    y2.start()
    y2.wait()
    full[z] = (total[...] + ybuf[...]) / den[z]

    def spread(step, d):
        block = lax.rem(z - step + nz, nz) if d == 0 else lax.rem(z + step, nz)
        ref = full.at[block]
        return remote(ref, ref, as_.at[d, step], ar.at[d, step], up if d == 0 else down)

    for d in range(2):
        spread(0, d).start()

    def spread_step(step, carry):
        for d in range(2):
            spread(step - 1, d).wait_recv()
            if d == 0:
                spread(step, d).start()
            else:
                @pl.when(step < half - 1)
                def _():
                    spread(step, d).start()
        return carry

    lax.fori_loop(1, half, spread_step, 0)
    spread(half - 1, 0).wait_recv()

    amp = full[pl.ds(0, half)].reshape(vir, vir)
    cross = full[pl.ds(half, half)].reshape(vir, vir)
    out_ref[...] = (
        dot(fac[...], amp, ((1,), (1,)))
        + 2.0 * dot(fj[...], cross, ((1,), (1,)))
        - dot(fj[...], cross, ((1,), (0,)))
    )

    def drain(step, carry):
        down_copy(step).wait_send()
        spread(step, 0).wait_send()

        @pl.when(step < half - 1)
        def _():
            up_copy(step).wait_send()
            spread(step, 1).wait_send()
        return carry

    lax.fori_loop(0, half, drain, 0)


def shards(nz, integrals, metric_root, occ_energy, virt_energy, partner):
    rows, _, vir = integrals.shape
    bits = 4
    half = nz // 2
    cut = 2 * vir // nz
    vm = pl.BlockSpec(memory_space=pltpu.VMEM)
    sm = pl.BlockSpec(memory_space=pltpu.SMEM)
    f32 = jnp.float32
    dma = pltpu.SemaphoreType.DMA
    out = pl.pallas_call(
        functools.partial(kernel, nz, bits, cut),
        out_shape=jax.ShapeDtypeStruct((rows, vir), f32),
        in_specs=[sm, sm, vm, vm, vm, vm],
        out_specs=vm,
        scratch_shapes=[
            pltpu.VMEM((nz, 2, rows, vir), f32),
            pltpu.VMEM((rows, vir), f32),
            pltpu.VMEM((rows, vir), f32),
            pltpu.VMEM((2 * bits, rows, vir), f32),
            pltpu.VMEM((nz, cut, vir), f32),
            pltpu.VMEM((nz, cut, vir), f32),
            pltpu.VMEM((half + 1, cut, vir), f32),
            pltpu.VMEM((half, cut, vir), f32),
            pltpu.VMEM((cut, vir), f32),
            pltpu.VMEM((nz, cut, vir), f32),
            pltpu.VMEM((cut, vir), f32),
            dma, dma,
            dma((2, 2, half)), dma((2, 2, half)),
            dma((bits,)), dma((bits,)),
            dma((half,)), dma((half,)),
            dma((half,)), dma((half,)),
            dma, dma,
            dma((2, half)), dma((2, half)),
        ],
        compiler_params=pltpu.CompilerParams(collective_id=0, has_side_effects=True),
    )(
        partner, occ_energy, integrals.reshape(rows, vir), metric_root,
        virt_energy.reshape(1, vir), virt_energy.reshape(vir, 1),
    )
    return out.reshape(rows, 1, vir)


def solution(mesh):
    nz = mesh.shape["aux"] // 2
    in_specs = (P("aux", "pair", None), P("aux", None), P(), P(), P())
    return jax.shard_map(
        functools.partial(shards, nz), mesh=mesh, in_specs=in_specs,
        out_specs=P("aux", "pair", None), check_vma=False,
    )
```

time: 513 us -> 136 us (0.27)
  waiting for transfers between devices: 475 us -> 0 us
  Pallas kernels: 0 us -> 131 us
  between operations: 16.7 us -> 0.01 us
  matrix products: 7.93 us -> 0 us
  starting transfers between devices: 5.29 us -> 0 us
    psum x1 -> x0, waiting for transfers between devices: 304 us -> none  [sum_round(): return lax.psum(partial_term, 'aux')]
    all_gather x1 -> x0, waiting for transfers between devices: 164 us -> none  [shards(): lax.all_gather(flat_rows, 'aux', axis=0, tiled=True)]
    pallas_call x0 -> x1, Pallas kernels: none -> 131 us  [shards(): pl.pallas_call(functools.partial(kernel, nz, bits, cut), out_shape=jax.Sh...]
    dot_general x5 -> x0, matrix products: 7.93 us -> none  [the longest x2 3.68 us: partial_pair(): lax.dot_general(own_rows, partner_rows, (((0,), (0,)), ((), ())), precisi...]
    all_gather x1 -> x0, local copies, waits for them, and re-layouts: 7 us -> none  [shards(): lax.all_gather(flat_rows, 'aux', axis=0, tiled=True)]
    ppermute x2 -> x0, waiting for transfers between devices: 6.26 us -> none  [partner_2(): return lax.ppermute(value, axis, pairs)]
    ppermute x2 -> x0, starting transfers between devices: 5.25 us -> none  [partner_2(): return lax.ppermute(value, axis, pairs)]
  transfers between devices with their start and end apart: 4 -> 0, of which waited for: 4 -> 0; matrix products, arithmetic and copies ran while one was open for 0% -> 0% of each run, Pallas kernels for 0% -> 0%
where the time goes in v1:
time: 136 us
  Pallas kernels  131 us (96%)
  local copies, waits for them, and re-layouts  5.22 us (4%)
    pallas_call x1, Pallas kernels, shards(): pl.pallas_call(functools.partial(kernel, nz, bits, cut), out_shape=jax.Sh...  131 us

profile of v1, /device:TPU:6, one launch (start us, length us, event | category | flops | bytes accessed | tf_op | source)
XLA Modules:
  0.0 136.1 jit_solution(13313561729857085418)
XLA Ops:
  0.0 1.3 reshape.13.vrow_ref
  1.3 0.0 copy-start
  1.3 1.6 %copy.11 = f32[64,1,320]{2,0,1:T(8,128)} copy(f32[64,1,320]{2,1,0:T(1,128)} %param.5) | data formatting | bytes 163840
  2.8 0.0 copy-done
  2.8 0.8 reshape.16.vcol_ref
  3.6 130.8 %shard_map.55 = f32[64,320]{1,0:T(8,128)} custom-call(s32[1,16]{1,0:T(1,128)} %partner_ref.1, f32[16]{0:T(128)} %occ_ref.1, f32[64,320]{1,0:T(8,128)} %bitcast.5, f32[64,2048]{1,0:T(8,128)} %metric_ref.1, f32[1,320]{1,0:T(1,128)} %reshape.13.vrow_ref, f32[320,1]{1,0:T(8,128)} %reshape.16.vcol_ref), custom_call_target="tpu_custom_call" | custom-call | tf_op jit(solution)/shard_map/pallas_call | solution.py:215
  134.4 1.6 %copy.8 = f32[64,1,320]{2,1,0:T(1,128)} copy(f32[64,1,320]{2,0,1:T(8,128)} %bitcast.4) | data formatting | bytes 163840 | tf_op jit(solution)/shard_map/reshape | solution.py:245
Async XLA Ops:
  1.3 1.6 %copy-start = (f32[320]{0:T(512)S(1)}, f32[320]{0:T(512)}, u32[]{:S(2)}) copy-start(f32[320]{0:T(512)} %param.8) | copy-start | bytes 3844

commit v2 on v1

v2 whole, which is shorter than its diff:
```python
import functools

import jax
import jax.numpy as jnp
from jax import lax
from jax.experimental import pallas as pl
from jax.experimental.pallas import tpu as pltpu
from jax.sharding import PartitionSpec as P

MESH = pl.DeviceIdType.MESH
HIGHEST = lax.Precision.HIGHEST


def flip(index, bit):
    return index + bit - 2 * bit * ((index // bit) % 2)


def dot(left, right, dims):
    return lax.dot_general(
        left, right, (dims, ((), ())), precision=HIGHEST, preferred_element_type=jnp.float32
    )


def kernel(
    nz, bits,
    partner_ref, occ_ref, ints_ref, metric_ref, vrow_ref, vcol_ref, out_ref,
    gat, fac, f4, ft4, bf, fj, fjt, fjt4, tq, rb, aq, den, amp,
    y_s, y_r, gs, gr, bs, br, fs, fr, js, jr, rs, rr, cs, cr, ds, dr,
):
    aux = lax.axis_index("aux")
    pair = lax.axis_index("pair")
    z = aux // 2
    yh = aux % 2
    rows, vir = ints_ref.shape
    up = lax.rem(z + 1, nz) * 2 + yh
    down = lax.rem(z + nz - 1, nz) * 2 + yh
    across = z * 2 + 1 - yh
    half = nz // 2
    far = nz // 2
    group = aux // 4
    q = aux % 4
    quarter = vir // 4
    used = quarter * 5 // 2
    part = tq.shape[1] // far
    mates = [group * 4 + lax.rem(q + k, 4) for k in range(1, 4)]
    remotes = [lax.rem(group + k, far) * 4 + q for k in range(1, far)]

    barrier = pltpu.get_barrier_semaphore()
    for other in [up, down] + mates + remotes:
        pl.semaphore_signal(barrier, inc=1, device_id={"aux": other, "pair": pair}, device_id_type=MESH)
    for b in range(bits):
        pl.semaphore_signal(barrier, inc=1, device_id={"aux": aux, "pair": flip(pair, 2**b)}, device_id_type=MESH)
    pl.semaphore_wait(barrier, 4 + far + bits)

    def remote(src, dst, s, r, dev_aux, dev_pair=None):
        return pltpu.make_async_remote_copy(
            src_ref=src, dst_ref=dst, send_sem=s, recv_sem=r,
            device_id={"aux": dev_aux, "pair": pair if dev_pair is None else dev_pair},
            device_id_type=MESH,
        )

    mine = gat.at[z, yh]
    ycopy = remote(ints_ref, mine, y_s, y_r, across)
    ycopy.start()

    def ring(step, d, h):
        block = lax.rem(z - step + nz, nz) if d == 0 else lax.rem(z + step, nz)
        ref = gat.at[block, yh if h == 0 else 1 - yh]
        src = ints_ref if h == 0 and isinstance(step, int) and step == 0 else ref
        return remote(src, ref, gs.at[d, h, step], gr.at[d, h, step], up if d == 0 else down)

    def arrived(step, d):
        return lax.rem(z - step - 1 + nz, nz) if d == 0 else lax.rem(z + step + 1, nz)

    def accumulate(block):
        columns = pl.ds(pl.multiple_of(block * 2 * rows, 2 * rows), 2 * rows)
        fac[...] += dot(metric_ref[:, columns], gat[block].reshape(2 * rows, vir), ((1,), (0,)))

    for d in range(2):
        ring(0, d, 0).start()
    mine[...] = ints_ref[...]
    fac[...] = jnp.zeros_like(fac)
    tq[...] = jnp.zeros_like(tq)
    den[...] = jnp.full(den.shape, -1.0, jnp.float32)
    own_rows = vcol_ref[pl.ds(q * quarter, quarter)]
    short = quarter // 2
    for which in range(2):
        own = occ_ref[pair]
        e = own + own if which == 0 else own + occ_ref[partner_ref[0, pair]]
        for c in range(2):
            den[which, c * quarter:(c + 1) * quarter] = e - own_rows - vrow_ref[:, c * 128:(c + 1) * 128]
        tail = vrow_ref[:, 256:vir]
        den[which, 2 * quarter:used] = jnp.concatenate(
            [e - own_rows[:short] - tail, e - own_rows[short:] - tail], axis=1
        )
    ycopy.wait()
    for d in range(2):
        ring(0, d, 1).start()
    accumulate(z)

    def gather_step(step, carry):
        for h in range(2):
            for d in range(2):
                ring(step - 1, d, h).wait_recv()
                if d == 0:
                    ring(step, d, h).start()
                else:
                    @pl.when(step < half - 1)
                    def _():
                        ring(step, d, h).start()
        for d in range(2):
            accumulate(arrived(step - 1, d))
        return carry

    lax.fori_loop(1, half, gather_step, 0)
    for h in range(2):
        ring(half - 1, 0, h).wait_recv()
    accumulate(arrived(half - 1, 0))

    f_copies = [
        remote(fac, f4.at[q], fs.at[k], fr.at[k], mates[k]) for k in range(3)
    ]
    b_copies = [
        remote(fac if b == 0 else bf.at[2 * b], bf.at[2 * b + 1], bs.at[b], br.at[b], aux, flip(pair, 2**b))
        for b in range(bits)
    ]
    b_copies[0].start()
    for copy in f_copies:
        copy.start()
    f4[q] = fac[...]
    mask = partner_ref[0, 0]

    def choose(b):
        b_copies[b].wait_recv()
        bit = (mask // 2**b) % 2
        kept = fac[...] if b == 0 else bf[2 * b]
        chosen = jnp.where(bit == 1, bf[2 * b + 1], kept)
        if b < bits - 1:
            bf[2 * b + 2] = chosen
            b_copies[b + 1].start()
        else:
            fj[...] = chosen

    def put(h, value):
        for c in range(2):
            tq[h, c * quarter:(c + 1) * quarter] = value[:, c * 128:(c + 1) * 128]
        tq[h, 2 * quarter:used] = jnp.concatenate([value[:short, 256:], value[short:, 256:]], axis=1)

    def piece(u):
        return pl.ds(pl.multiple_of(u * part, 8), part)

    def scatter(h, k):
        to = lax.rem(group + k, far)
        return remote(tq.at[h, piece(to)], rb.at[h, k - 1], rs.at[h, k - 1], rr.at[h, k - 1], remotes[k - 1])

    def reduce(h):
        value = tq[h, piece(group)]
        for k in range(1, far):
            scatter(h, k).wait_recv()
            value = value + rb[h, k - 1]
        aq[h, q, piece(group)] = value / den[h, piece(group)]

    def spread(h, k):
        ref = aq.at[h, q, piece(group)]
        return remote(ref, ref, cs.at[h, k - 1], cr.at[h, k - 1], remotes[k - 1])

    def hand(h, k, m):
        ref = aq.at[h, q, piece(lax.rem(group - k + far, far))]
        return remote(ref, ref, ds.at[h, k, m], dr.at[h, k, m], mates[m])

    order = [k for pair_ in zip(range(1, far // 2 + 1), range(far - 1, far // 2 - 1, -1)) for k in pair_]
    order = list(dict.fromkeys(order))

    for b in range(bits - 1):
        choose(b)
    for m in range(3):
        f_copies[m].wait_recv()
    sum_ii = jnp.zeros((quarter, vir), jnp.float32)
    for src in range(4):
        ft4[src] = f4[src].T
        sum_ii += dot(ft4[src, pl.ds(pl.multiple_of(q * quarter, 8), quarter)], f4[src], ((1,), (0,)))
    put(0, sum_ii)
    for k in order[::-1]:
        scatter(0, k).start()
    choose(bits - 1)
    fjt[...] = fj[...].T
    j_copies = []
    for k in range(3):
        to = lax.rem(q + 1 + k, 4)
        j_copies.append(remote(
            fjt.at[pl.ds(pl.multiple_of(to * quarter, 8), quarter)], fjt4.at[q], js.at[k], jr.at[k], mates[k]
        ))
        j_copies[k].start()
    fjt4[q] = fjt[pl.ds(pl.multiple_of(q * quarter, 8), quarter)]
    for k in range(3):
        j_copies[k].wait_recv()
    sum_ij = jnp.zeros((quarter, vir), jnp.float32)
    for src in range(4):
        sum_ij += dot(fjt4[src], f4[src], ((1,), (0,)))
    put(1, sum_ij)
    for k in order[::-1]:
        scatter(1, k).start()
    for h in range(2):
        reduce(h)
        for k in order[::-1]:
            spread(h, k).start()
        for m in range(3):
            hand(h, 0, m).start()
    for h in range(2):
        for k in order:
            spread(h, k).wait_recv()
            for m in range(3):
                hand(h, k, m).start()
    for h in range(2):
        for k in range(far):
            for m in range(3):
                hand(h, k, m).wait_recv()
        for g in range(4):
            for c in range(2):
                amp[h, g * quarter:(g + 1) * quarter, c * 128:(c + 1) * 128] = (
                    aq[h, g, c * quarter:(c + 1) * quarter]
                )
            for c in range(2):
                amp[h, g * quarter + c * short:g * quarter + (c + 1) * short, 256:vir] = (
                    aq[h, g, 2 * quarter:used, c * 64:(c + 1) * 64]
                )
        if h == 0:
            out_ref[...] = dot(fac[...], amp[0], ((1,), (0,)))
        else:
            out_ref[...] += (
                2.0 * dot(fj[...], amp[1], ((1,), (0,))) - dot(fj[...], amp[1], ((1,), (1,)))
            )

    def gather_drain(step, carry):
        for h in range(2):
            ring(step, 0, h).wait_send()

            @pl.when(step < half - 1)
            def _():
                ring(step, 1, h).wait_send()
        return carry

    lax.fori_loop(0, half, gather_drain, 0)
    for copy in f_copies + b_copies + j_copies:
        copy.wait_send()
    for h in range(2):
        for k in range(1, far):
            scatter(h, k).wait_send()
            spread(h, k).wait_send()
        for k in range(far):
            for m in range(3):
                hand(h, k, m).wait_send()


def shards(nz, integrals, metric_root, occ_energy, virt_energy, partner):
    rows, _, vir = integrals.shape
    bits = 4
    half = nz // 2
    far = nz // 2
    quarter = vir // 4
    padded = -(-(quarter * 5 // 2) // (8 * far)) * 8 * far
    vm = pl.BlockSpec(memory_space=pltpu.VMEM)
    sm = pl.BlockSpec(memory_space=pltpu.SMEM)
    f32 = jnp.float32
    dma = pltpu.SemaphoreType.DMA
    out = pl.pallas_call(
        functools.partial(kernel, nz, bits),
        out_shape=jax.ShapeDtypeStruct((rows, vir), f32),
        in_specs=[sm, sm, vm, vm, vm, vm],
        out_specs=vm,
        scratch_shapes=[
            pltpu.VMEM((nz, 2, rows, vir), f32),
            pltpu.VMEM((rows, vir), f32),
            pltpu.VMEM((4, rows, vir), f32),
            pltpu.VMEM((4, vir, rows), f32),
            pltpu.VMEM((2 * bits, rows, vir), f32),
            pltpu.VMEM((rows, vir), f32),
            pltpu.VMEM((vir, rows), f32),
            pltpu.VMEM((4, quarter, rows), f32),
            pltpu.VMEM((2, padded, 128), f32),
            pltpu.VMEM((2, far - 1, padded // far, 128), f32),
            pltpu.VMEM((2, 4, padded, 128), f32),
            pltpu.VMEM((2, padded, 128), f32),
            pltpu.VMEM((2, vir, vir), f32),
            dma, dma,
            dma((2, 2, half)), dma((2, 2, half)),
            dma((bits,)), dma((bits,)),
            dma((3,)), dma((3,)),
            dma((3,)), dma((3,)),
            dma((2, far - 1)), dma((2, far - 1)),
            dma((2, far - 1)), dma((2, far - 1)),
            dma((2, far, 3)), dma((2, far, 3)),
        ],
        compiler_params=pltpu.CompilerParams(collective_id=0, has_side_effects=True),
    )(
        partner, occ_energy, integrals.reshape(rows, vir), metric_root,
        virt_energy.reshape(1, vir), virt_energy.reshape(vir, 1),
    )
    return out.reshape(rows, 1, vir)


def solution(mesh):
    nz = mesh.shape["aux"] // 2
    in_specs = (P("aux", "pair", None), P("aux", None), P(), P(), P())
    return jax.shard_map(
        functools.partial(shards, nz), mesh=mesh, in_specs=in_specs,
        out_specs=P("aux", "pair", None), check_vma=False,
    )
```

time: 136 us -> 117 us (0.86)
  Pallas kernels: 131 us -> 111 us
    pallas_call x1, Pallas kernels: 131 us -> 111 us  [shards(): pl.pallas_call(functools.partial(kernel, nz, bits), out_shape=jax.ShapeDt...]
where the time goes in v2:
time: 117 us; the launch traced here: 116 us
  Pallas kernels  111 us (95%)
  local copies, waits for them, and re-layouts  5.22 us (4%)
    pallas_call x1, Pallas kernels, shards(): pl.pallas_call(functools.partial(kernel, nz, bits), out_shape=jax.ShapeDt...  111 us

profile of v2, /device:TPU:6, one launch (start us, length us, event | category | flops | bytes accessed | tf_op | source)
XLA Modules:
  0.0 115.9 jit_solution(11603856086764086068)
XLA Ops:
  0.0 1.3 %reshape.13.vrow_ref = f32[1,320]{1,0:T(1,128)} reshape(f32[320]{0:T(512)} %param.8) | data formatting | bytes 2560 | tf_op jit(solution)/shard_map/reshape | solution.py:297
  1.3 0.0 copy-start
  1.3 1.6 %copy.11 = f32[64,1,320]{2,0,1:T(8,128)} copy(f32[64,1,320]{2,1,0:T(1,128)} %param.5) | data formatting | bytes 163840
  2.8 0.0 copy-done
  2.8 0.8 reshape.16.vcol_ref
  3.6 110.7 %shard_map.55 = f32[64,320]{1,0:T(8,128)} custom-call(s32[1,16]{1,0:T(1,128)} %partner_ref.1, f32[16]{0:T(128)} %occ_ref.1, f32[64,320]{1,0:T(8,128)} %bitcast.5, f32[64,2048]{1,0:T(8,128)} %metric_ref.1, f32[1,320]{1,0:T(1,128)} %reshape.13.vrow_ref, f32[320,1]{1,0:T(8,128)} %reshape.16.vcol_ref), custom_call_target="tpu_custom_call" | custom-call | tf_op jit(solution)/shard_map/pallas_call | solution.py:266
  114.3 1.6 %copy.8 = f32[64,1,320]{2,1,0:T(1,128)} copy(f32[64,1,320]{2,0,1:T(8,128)} %bitcast.4) | data formatting | bytes 163840 | tf_op jit(solution)/shard_map/reshape | solution.py:299
Async XLA Ops:
  1.3 1.6 %copy-start = (f32[320]{0:T(512)S(1)}, f32[320]{0:T(512)}, u32[]{:S(2)}) copy-start(f32[320]{0:T(512)} %param.8) | copy-start | bytes 3844

commit v3 on v2

v3 whole, which is shorter than its diff:
```python
import functools

import jax
import jax.numpy as jnp
from jax import lax
from jax.experimental import pallas as pl
from jax.experimental.pallas import tpu as pltpu
from jax.sharding import PartitionSpec as P

MESH = pl.DeviceIdType.MESH

def flip(index, bit):
    return index + bit - 2 * bit * ((index // bit) % 2)


def split(value):
    high = value.astype(jnp.bfloat16)
    return high, (value - high.astype(jnp.float32)).astype(jnp.bfloat16)


def dot(left, right, dims):
    l_high, l_low = split(left)
    r_high, r_low = split(right)
    one = functools.partial(
        lax.dot_general, dimension_numbers=(dims, ((), ())), preferred_element_type=jnp.float32
    )
    return one(l_high, r_high) + (one(l_high, r_low) + one(l_low, r_high))


def pack(value):
    short = value.shape[0] // 2
    tail = jnp.concatenate([value[:short, 256:], value[short:, 256:]], axis=1)
    return jnp.concatenate([value[:, :128], value[:, 128:256], tail], axis=0)


def unpack(value):
    rows = value.shape[0] * 2 // 5
    tail = jnp.concatenate([value[2 * rows:, :64], value[2 * rows:, 64:]], axis=0)
    return jnp.concatenate([value[:rows], value[rows:2 * rows], tail], axis=1)


def kernel(
    nz, bits,
    partner_ref, occ_ref, ints_ref, metric_ref, virt_ref, out_ref,
    gat, metric2, select, wide, yout, yin, fac, f4p, f4, ft, bf, fj, fjt, fjt4, tq, rb, aq, den, amp, vcol,
    m_s, m_r, y_s, y_r, es, er, os_, or_, bs, br, fs, fr, js, jr, rs, rr, cs, cr, ds, dr,
):
    aux = lax.axis_index("aux")
    pair = lax.axis_index("pair")
    z = aux // 2
    yh = aux % 2
    rows, _, vir = ints_ref.shape
    up = lax.rem(z + 1, nz) * 2 + yh
    down = lax.rem(z + nz - 1, nz) * 2 + yh
    across = z * 2 + 1 - yh
    half = nz // 2
    far = nz // 2
    group = aux // 4
    q = aux % 4
    quarter = vir // 4
    used = quarter * 5 // 2
    part = tq.shape[1] // far
    mates = [group * 4 + lax.rem(q + k, 4) for k in range(1, 4)]
    remotes = [lax.rem(group + k, far) * 4 + q for k in range(1, far)]

    barrier = pltpu.get_barrier_semaphore()
    for other in [up, down] + mates + remotes:
        pl.semaphore_signal(barrier, inc=1, device_id={"aux": other, "pair": pair}, device_id_type=MESH)
    for b in range(bits):
        pl.semaphore_signal(barrier, inc=1, device_id={"aux": aux, "pair": flip(pair, 2**b)}, device_id_type=MESH)
    pl.semaphore_wait(barrier, 4 + far + bits)

    def remote(src, dst, s, r, dev_aux, dev_pair=None):
        return pltpu.make_async_remote_copy(
            src_ref=src, dst_ref=dst, send_sem=s, recv_sem=r,
            device_id={"aux": dev_aux, "pair": pair if dev_pair is None else dev_pair},
            device_id_type=MESH,
        )

    m_copy = remote(metric_ref, metric2, m_s, m_r, across)
    gat[z] = pack(ints_ref[:, 0, :])

    def relay(d, k):
        block = lax.rem(z - 2 * k + 2 * nz, nz) if d == 0 else lax.rem(z + 2 * k, nz)
        ref = gat.at[block]
        if k == half // 2 - 1:
            size = gat.shape[1] // 2
            ref = gat.at[block, pl.ds(d * size, size)]
        return remote(ref, ref, es.at[d, k], er.at[d, k], remotes[0] if d == 0 else remotes[-1])

    def side(d, k):
        block = lax.rem(z - 2 * k + 2 * nz, nz) if d == 0 else lax.rem(z + 2 * k, nz)
        ref = gat.at[block]
        return remote(ref, ref, os_.at[d, k], or_.at[d, k], up if d == 0 else down)

    steps = half // 2
    for d in range(2):
        relay(d, 0).start()
    for d in range(2):
        side(d, 0).start()
    m_copy.start()

    def choose_columns(ref, base):
        for b in range(nz):
            both = ref[:, b * 2 * rows:(b + 1) * 2 * rows]
            select[b, base:base + rows] = jnp.where(yh == 0, both[:, :rows], both[:, rows:])

    choose_columns(metric_ref, 0)
    wide[...] = jnp.zeros_like(wide)
    tq[...] = jnp.zeros_like(tq)
    den[...] = jnp.full(den.shape, -1.0, jnp.float32)
    v_row = virt_ref[...].reshape(1, vir)
    vcol[...] = jnp.broadcast_to(v_row, (8, vir)).T
    own_rows = vcol[pl.ds(pl.multiple_of(q * quarter, 8), quarter), :1]
    short = quarter // 2
    for which in range(2):
        own = occ_ref[pair]
        e = own + own if which == 0 else own + occ_ref[partner_ref[0, pair]]
        den[which, :used] = pack(e - own_rows - v_row)

    for k in range(1, steps):
        for d in range(2):
            relay(d, k - 1).wait_recv()
            relay(d, k).start()
        for d in range(2):
            side(d, k).start()

    def accumulate(block):
        wide[...] += dot(select[block], unpack(gat[block]), ((1,), (0,)))

    m_copy.wait_recv()
    choose_columns(metric2, rows)
    accumulate(z)
    for k in range(steps):
        for d in range(2):
            side(d, k).wait_recv()
            away = 2 * k + 1
            accumulate(lax.rem(z - away + nz, nz) if d == 0 else lax.rem(z + away, nz))
        if k < steps - 1:
            for d in range(2):
                away = 2 * k + 2
                accumulate(lax.rem(z - away + nz, nz) if d == 0 else lax.rem(z + away, nz))
    for d in range(2):
        relay(d, steps - 1).wait_recv()
    accumulate(lax.rem(z + half, nz))
    yout[...] = pack(wide[rows:])
    y_copy = remote(yout, yin, y_s, y_r, across)
    y_copy.start()
    y_copy.wait_recv()
    fac[...] = wide[:rows] + unpack(yin[...])
    bf[0] = pack(fac[...])

    f_copies = [
        remote(bf.at[0], f4p.at[q], fs.at[k], fr.at[k], mates[k]) for k in range(3)
    ]
    b_copies = [
        remote(bf.at[2 * b], bf.at[2 * b + 1], bs.at[b], br.at[b], aux, flip(pair, 2**b))
        for b in range(bits)
    ]
    b_copies[0].start()
    for copy in f_copies:
        copy.start()
    f4p[q] = bf[0]
    mask = partner_ref[0, 0]

    def choose(b):
        b_copies[b].wait_recv()
        bit = (mask // 2**b) % 2
        chosen = jnp.where(bit == 1, bf[2 * b + 1], bf[2 * b])
        if b < bits - 1:
            bf[2 * b + 2] = chosen
            b_copies[b + 1].start()
        else:
            fj[...] = unpack(chosen)

    def put(h, value):
        tq[h, :used] = pack(value)

    def piece(u):
        return pl.ds(pl.multiple_of(u * part, 8), part)

    def scatter(h, k):
        to = lax.rem(group + k, far)
        return remote(tq.at[h, piece(to)], rb.at[h, k - 1], rs.at[h, k - 1], rr.at[h, k - 1], remotes[k - 1])

    def reduce(h):
        value = tq[h, piece(group)]
        for k in range(1, far):
            scatter(h, k).wait_recv()
            value = value + rb[h, k - 1]
        aq[h, q, piece(group)] = value / den[h, piece(group)]

    def spread(h, k):
        ref = aq.at[h, q, piece(group)]
        return remote(ref, ref, cs.at[h, k - 1], cr.at[h, k - 1], remotes[k - 1])

    def hand(h, k, m):
        ref = aq.at[h, q, piece(lax.rem(group - k + far, far))]
        return remote(ref, ref, ds.at[h, k, m], dr.at[h, k, m], mates[m])

    order = [k for pair_ in zip(range(1, far // 2 + 1), range(far - 1, far // 2 - 1, -1)) for k in pair_]
    order = list(dict.fromkeys(order))

    for b in range(bits - 1):
        choose(b)
    for m in range(3):
        f_copies[m].wait_recv()
    for src in range(4):
        f4[src * rows:(src + 1) * rows] = unpack(f4p[src])
    ft[...] = f4[...].T
    own_quarter = pl.ds(pl.multiple_of(q * quarter, 8), quarter)
    sum_ii = dot(ft[own_quarter], f4[...], ((1,), (0,)))
    put(0, sum_ii)
    for k in order[::-1]:
        scatter(0, k).start()
    choose(bits - 1)
    fjt[...] = fj[...].T
    j_copies = []
    for k in range(3):
        to = lax.rem(q + 1 + k, 4)
        j_copies.append(remote(
            fjt.at[pl.ds(pl.multiple_of(to * quarter, 8), quarter)], fjt4.at[q], js.at[k], jr.at[k], mates[k]
        ))
        j_copies[k].start()
    fjt4[q] = fjt[pl.ds(pl.multiple_of(q * quarter, 8), quarter)]
    for k in range(3):
        j_copies[k].wait_recv()
    partner_t = jnp.concatenate([fjt4[src] for src in range(4)], axis=1)
    sum_ij = dot(partner_t, f4[...], ((1,), (0,)))
    put(1, sum_ij)
    for k in order[::-1]:
        scatter(1, k).start()
    for h in range(2):
        reduce(h)
        for k in order[::-1]:
            spread(h, k).start()
        for m in range(3):
            hand(h, 0, m).start()
    for h in range(2):
        for k in order:
            spread(h, k).wait_recv()
            for m in range(3):
                hand(h, k, m).start()
    for h in range(2):
        for k in range(far):
            for m in range(3):
                hand(h, k, m).wait_recv()
        for g in range(4):
            amp[h, g * quarter:(g + 1) * quarter] = unpack(aq[h, g, :used])
        if h == 0:
            first = dot(fac[...], amp[0], ((1,), (0,)))
        else:
            out_ref[:, 0, :] = first + (
                2.0 * dot(fj[...], amp[1], ((1,), (0,))) - dot(fj[...], amp[1], ((1,), (1,)))
            )

    for d in range(2):
        for k in range(steps):
            relay(d, k).wait_send()
            side(d, k).wait_send()
    for copy in [m_copy, y_copy] + f_copies + b_copies + j_copies:
        copy.wait_send()
    for h in range(2):
        for k in range(1, far):
            scatter(h, k).wait_send()
            spread(h, k).wait_send()
        for k in range(far):
            for m in range(3):
                hand(h, k, m).wait_send()


def shards(nz, integrals, metric_root, occ_energy, virt_energy, partner):
    rows, _, vir = integrals.shape
    bits = 4
    half = nz // 2
    far = nz // 2
    quarter = vir // 4
    packed = rows * 5 // 2
    padded = -(-(quarter * 5 // 2) // (8 * far)) * 8 * far
    vm = pl.BlockSpec(memory_space=pltpu.VMEM)
    sm = pl.BlockSpec(memory_space=pltpu.SMEM)
    f32 = jnp.float32
    dma = pltpu.SemaphoreType.DMA
    out = pl.pallas_call(
        functools.partial(kernel, nz, bits),
        out_shape=jax.ShapeDtypeStruct((rows, 1, vir), f32),
        in_specs=[sm, sm, vm, vm, vm],
        out_specs=vm,
        scratch_shapes=[
            pltpu.VMEM((nz, packed, 128), f32),
            pltpu.VMEM(metric_root.shape, f32),
            pltpu.VMEM((nz, 2 * rows, rows), f32),
            pltpu.VMEM((2 * rows, vir), f32),
            pltpu.VMEM((packed, 128), f32),
            pltpu.VMEM((packed, 128), f32),
            pltpu.VMEM((rows, vir), f32),
            pltpu.VMEM((4, packed, 128), f32),
            pltpu.VMEM((4 * rows, vir), f32),
            pltpu.VMEM((vir, 4 * rows), f32),
            pltpu.VMEM((2 * bits, packed, 128), f32),
            pltpu.VMEM((rows, vir), f32),
            pltpu.VMEM((vir, rows), f32),
            pltpu.VMEM((4, quarter, rows), f32),
            pltpu.VMEM((2, padded, 128), f32),
            pltpu.VMEM((2, far - 1, padded // far, 128), f32),
            pltpu.VMEM((2, 4, padded, 128), f32),
            pltpu.VMEM((2, padded, 128), f32),
            pltpu.VMEM((2, vir, vir), f32),
            pltpu.VMEM((vir, 8), f32),
            dma, dma,
            dma, dma,
            dma((2, half // 2)), dma((2, half // 2)),
            dma((2, half // 2)), dma((2, half // 2)),
            dma((bits,)), dma((bits,)),
            dma((3,)), dma((3,)),
            dma((3,)), dma((3,)),
            dma((2, far - 1)), dma((2, far - 1)),
            dma((2, far - 1)), dma((2, far - 1)),
            dma((2, far, 3)), dma((2, far, 3)),
        ],
        compiler_params=pltpu.CompilerParams(collective_id=0, has_side_effects=True),
    )(
        partner, occ_energy, integrals, metric_root, virt_energy,
    )
    return out


def solution(mesh):
    nz = mesh.shape["aux"] // 2
    in_specs = (P("aux", "pair", None), P("aux", None), P(), P(), P())
    return jax.shard_map(
        functools.partial(shards, nz), mesh=mesh, in_specs=in_specs,
        out_specs=P("aux", "pair", None), check_vma=False,
    )
```

time: 117 us -> 102 us (0.87)
  the two profiles are of different devices: /device:TPU:6 before, /device:TPU:1 now
where the time goes in v3:
time: 102 us
  Pallas kernels  100 us (98%)
  local copies, waits for them, and re-layouts  1.58 us (2%)
    pallas_call x1, Pallas kernels, shards(): pl.pallas_call(functools.partial(kernel, nz, bits), out_shape=jax.ShapeDt...  100 us

profile of v3, /device:TPU:1, one launch (start us, length us, event | category | flops | bytes accessed | tf_op | source)
XLA Modules:
  0.0 101.6 jit_solution(17805596465022277546)
XLA Ops:
  0.0 100.0 %shard_map.55 = f32[64,1,320]{2,1,0:T(1,128)} custom-call(s32[1,16]{1,0:T(1,128)} %partner_ref.1, f32[16]{0:T(128)} %occ_ref.1, f32[64,1,320]{2,1,0:T(1,128)} %ints_ref.1, f32[64,2048]{1,0:T(8,128)} %metric_ref.1, f32[320]{0:T(512)} %virt_ref.1), custom_call_target="tpu_custom_call" | custom-call | tf_op jit(solution)/shard_map/pallas_call | solution.py:284
  100.0 1.6 %copy.7 = f32[64,1,320]{2,1,0:T(1,128)} copy(f32[64,1,320]{2,1,0:T(1,128)} %shard_map.55) | data formatting | bytes 163840

commit v4 on v3

--- a/solution.py
+++ b/solution.py
@@ -42,8 +42,8 @@
 def kernel(
     nz, bits,
     partner_ref, occ_ref, ints_ref, metric_ref, virt_ref, out_ref,
-    gat, metric2, select, wide, yout, yin, fac, f4p, f4, ft, bf, fj, fjt, fjt4, tq, rb, aq, den, amp, vcol,
-    m_s, m_r, y_s, y_r, es, er, os_, or_, bs, br, fs, fr, js, jr, rs, rr, cs, cr, ds, dr,
+    gat, metric2, select, wide, yout, yin, f4p, f4, ft, bf, j4p, j4, jt, tq, rb, aq, den, part, pout, pin, vcol,
+    m_s, m_r, y_s, y_r, es, er, os_, or_, bs, br, fs, fr, js, jr, rs, rr, cs, cr, ps, pr,
 ):
     aux = lax.axis_index("aux")
     pair = lax.axis_index("pair")
@@ -59,7 +59,7 @@
     q = aux % 4
     quarter = vir // 4
     used = quarter * 5 // 2
-    part = tq.shape[1] // far
+    span = tq.shape[1] // far
     mates = [group * 4 + lax.rem(q + k, 4) for k in range(1, 4)]
     remotes = [lax.rem(group + k, far) * 4 + q for k in range(1, far)]
 
@@ -147,8 +147,7 @@
     y_copy = remote(yout, yin, y_s, y_r, across)
     y_copy.start()
     y_copy.wait_recv()
-    fac[...] = wide[:rows] + unpack(yin[...])
-    bf[0] = pack(fac[...])
+    bf[0] = pack(wide[:rows]) + yin[...]
 
     f_copies = [
         remote(bf.at[0], f4p.at[q], fs.at[k], fr.at[k], mates[k]) for k in range(3)
@@ -167,17 +166,15 @@
         b_copies[b].wait_recv()
         bit = (mask // 2**b) % 2
         chosen = jnp.where(bit == 1, bf[2 * b + 1], bf[2 * b])
+        bf[2 * b + 2] = chosen
         if b < bits - 1:
-            bf[2 * b + 2] = chosen
             b_copies[b + 1].start()
-        else:
-            fj[...] = unpack(chosen)
 
     def put(h, value):
         tq[h, :used] = pack(value)
 
     def piece(u):
-        return pl.ds(pl.multiple_of(u * part, 8), part)
+        return pl.ds(pl.multiple_of(u * span, 8), span)
 
     def scatter(h, k):
         to = lax.rem(group + k, far)
@@ -188,15 +185,11 @@
         for k in range(1, far):
             scatter(h, k).wait_recv()
             value = value + rb[h, k - 1]
-        aq[h, q, piece(group)] = value / den[h, piece(group)]
+        aq[h, piece(group)] = value / den[h, piece(group)]
 
     def spread(h, k):
-        ref = aq.at[h, q, piece(group)]
+        ref = aq.at[h, piece(group)]
         return remote(ref, ref, cs.at[h, k - 1], cr.at[h, k - 1], remotes[k - 1])
-
-    def hand(h, k, m):
-        ref = aq.at[h, q, piece(lax.rem(group - k + far, far))]
-        return remote(ref, ref, ds.at[h, k, m], dr.at[h, k, m], mates[m])
 
     order = [k for pair_ in zip(range(1, far // 2 + 1), range(far - 1, far // 2 - 1, -1)) for k in pair_]
     order = list(dict.fromkeys(order))
@@ -214,19 +207,16 @@
     for k in order[::-1]:
         scatter(0, k).start()
     choose(bits - 1)
-    fjt[...] = fj[...].T
-    j_copies = []
-    for k in range(3):
-        to = lax.rem(q + 1 + k, 4)
-        j_copies.append(remote(
-            fjt.at[pl.ds(pl.multiple_of(to * quarter, 8), quarter)], fjt4.at[q], js.at[k], jr.at[k], mates[k]
-        ))
-        j_copies[k].start()
-    fjt4[q] = fjt[pl.ds(pl.multiple_of(q * quarter, 8), quarter)]
-    for k in range(3):
-        j_copies[k].wait_recv()
-    partner_t = jnp.concatenate([fjt4[src] for src in range(4)], axis=1)
-    sum_ij = dot(partner_t, f4[...], ((1,), (0,)))
+    j_copies = [remote(bf.at[2 * bits], j4p.at[q], js.at[k], jr.at[k], mates[k]) for k in range(3)]
+    for copy in j_copies:
+        copy.start()
+    j4p[q] = bf[2 * bits]
+    for copy in j_copies:
+        copy.wait_recv()
+    for src in range(4):
+        j4[src * rows:(src + 1) * rows] = unpack(j4p[src])
+    jt[...] = j4[...].T
+    sum_ij = dot(jt[own_quarter], f4[...], ((1,), (0,)))
     put(1, sum_ij)
     for k in order[::-1]:
         scatter(1, k).start()
@@ -234,39 +224,40 @@
         reduce(h)
         for k in order[::-1]:
             spread(h, k).start()
-        for m in range(3):
-            hand(h, 0, m).start()
-    for h in range(2):
-        for k in order:
-            spread(h, k).wait_recv()
-            for m in range(3):
-                hand(h, k, m).start()
-    for h in range(2):
-        for k in range(far):
-            for m in range(3):
-                hand(h, k, m).wait_recv()
-        for g in range(4):
-            amp[h, g * quarter:(g + 1) * quarter] = unpack(aq[h, g, :used])
-        if h == 0:
-            first = dot(fac[...], amp[0], ((1,), (0,)))
-        else:
-            out_ref[:, 0, :] = first + (
-                2.0 * dot(fj[...], amp[1], ((1,), (0,))) - dot(fj[...], amp[1], ((1,), (1,)))
-            )
+    for k in order:
+        spread(0, k).wait_recv()
+    part[...] = dot(ft[own_quarter], unpack(aq[0, :used]), ((0,), (0,)))
+    for k in order:
+        spread(1, k).wait_recv()
+    cross = unpack(aq[1, :used])
+    part[...] += dot(2.0 * jt[own_quarter], cross, ((0,), (0,)))
+    swapped = dot(j4[...], cross, ((1,), (1,)))
+    for g in range(4):
+        @pl.when(q == g)
+        def _():
+            part[:, g * quarter:(g + 1) * quarter] -= swapped
+    p_copies = []
+    for k in range(3):
+        to = lax.rem(q + 1 + k, 4)
+        pout[k] = pack(part[pl.ds(pl.multiple_of(to * rows, 8), rows)])
+        p_copies.append(remote(pout.at[k], pin.at[k], ps.at[k], pr.at[k], mates[k]))
+        p_copies[k].start()
+    total = pack(part[pl.ds(pl.multiple_of(q * rows, 8), rows)])
+    for k in range(3):
+        p_copies[k].wait_recv()
+        total += pin[k]
+    out_ref[:, 0, :] = unpack(total)
 
     for d in range(2):
         for k in range(steps):
             relay(d, k).wait_send()
             side(d, k).wait_send()
-    for copy in [m_copy, y_copy] + f_copies + b_copies + j_copies:
+    for copy in [m_copy, y_copy] + f_copies + b_copies + j_copies + p_copies:
         copy.wait_send()
     for h in range(2):
         for k in range(1, far):
             scatter(h, k).wait_send()
             spread(h, k).wait_send()
-        for k in range(far):
-            for m in range(3):
-                hand(h, k, m).wait_send()
 
 
 def shards(nz, integrals, metric_root, occ_energy, virt_energy, partner):
@@ -293,19 +284,20 @@
             pltpu.VMEM((2 * rows, vir), f32),
             pltpu.VMEM((packed, 128), f32),
             pltpu.VMEM((packed, 128), f32),
-            pltpu.VMEM((rows, vir), f32),
             pltpu.VMEM((4, packed, 128), f32),
             pltpu.VMEM((4 * rows, vir), f32),
             pltpu.VMEM((vir, 4 * rows), f32),
-            pltpu.VMEM((2 * bits, packed, 128), f32),
-            pltpu.VMEM((rows, vir), f32),
-            pltpu.VMEM((vir, rows), f32),
-            pltpu.VMEM((4, quarter, rows), f32),
+            pltpu.VMEM((2 * bits + 1, packed, 128), f32),
+            pltpu.VMEM((4, packed, 128), f32),
+            pltpu.VMEM((4 * rows, vir), f32),
+            pltpu.VMEM((vir, 4 * rows), f32),
             pltpu.VMEM((2, padded, 128), f32),
             pltpu.VMEM((2, far - 1, padded // far, 128), f32),
-            pltpu.VMEM((2, 4, padded, 128), f32),
             pltpu.VMEM((2, padded, 128), f32),
-            pltpu.VMEM((2, vir, vir), f32),
+            pltpu.VMEM((2, padded, 128), f32),
+            pltpu.VMEM((4 * rows, vir), f32),
+            pltpu.VMEM((3, packed, 128), f32),
+            pltpu.VMEM((3, packed, 128), f32),
             pltpu.VMEM((vir, 8), f32),
             dma, dma,
             dma, dma,
@@ -316,7 +308,7 @@
             dma((3,)), dma((3,)),
             dma((2, far - 1)), dma((2, far - 1)),
             dma((2, far - 1)), dma((2, far - 1)),
-            dma((2, far, 3)), dma((2, far, 3)),
+            dma((3,)), dma((3,)),
         ],
         compiler_params=pltpu.CompilerParams(collective_id=0, has_side_effects=True),
     )(

time: 102 us -> 97 us (0.951)
  the two profiles are of different devices: /device:TPU:1 before, /device:TPU:6 now
where the time goes in v4:
time: 97 us; the launch traced here: 96.3 us
  Pallas kernels  94.7 us (98%)
  local copies, waits for them, and re-layouts  1.58 us (2%)
    pallas_call x1, Pallas kernels, shards(): pl.pallas_call(functools.partial(kernel, nz, bits), out_shape=jax.ShapeDt...  94.7 us

profile of v4, /device:TPU:6, one launch (start us, length us, event | category | flops | bytes accessed | tf_op | source)
XLA Modules:
  0.0 96.3 jit_solution(12839907880581904395)
XLA Ops:
  0.0 94.7 %shard_map.55 = f32[64,1,320]{2,1,0:T(1,128)} custom-call(s32[1,16]{1,0:T(1,128)} %partner_ref.1, f32[16]{0:T(128)} %occ_ref.1, f32[64,1,320]{2,1,0:T(1,128)} %ints_ref.1, f32[64,2048]{1,0:T(8,128)} %metric_ref.1, f32[320]{0:T(512)} %virt_ref.1), custom_call_target="tpu_custom_call" | custom-call | tf_op jit(solution)/shard_map/pallas_call | solution.py:275
  94.7 1.6 %copy.7 = f32[64,1,320]{2,1,0:T(1,128)} copy(f32[64,1,320]{2,1,0:T(1,128)} %shard_map.55) | data formatting | bytes 163840

commit v5 on v4

v5 whole, which is shorter than its diff:
```python
import functools

import jax
import jax.numpy as jnp
from jax import lax
from jax.experimental import pallas as pl
from jax.experimental.pallas import tpu as pltpu
from jax.sharding import PartitionSpec as P

MESH = pl.DeviceIdType.MESH

def flip(index, mask):
    for bit in (1, 2, 4, 8):
        if mask & bit:
            index = index + bit - 2 * bit * ((index // bit) % 2)
    return index


def split(value):
    high = value.astype(jnp.bfloat16)
    return high, (value - high.astype(jnp.float32)).astype(jnp.bfloat16)


def dot(left, right, dims):
    l_high, l_low = split(left)
    r_high, r_low = split(right)
    one = functools.partial(
        lax.dot_general, dimension_numbers=(dims, ((), ())), preferred_element_type=jnp.float32
    )
    return one(l_high, r_high) + (one(l_high, r_low) + one(l_low, r_high))


def pack(value):
    short = value.shape[0] // 2
    tail = jnp.concatenate([value[:short, 256:], value[short:, 256:]], axis=1)
    return jnp.concatenate([value[:, :128], value[:, 128:256], tail], axis=0)


def unpack(value):
    rows = value.shape[0] * 2 // 5
    tail = jnp.concatenate([value[2 * rows:, :64], value[2 * rows:, 64:]], axis=0)
    return jnp.concatenate([value[:rows], value[rows:2 * rows], tail], axis=1)


def kernel(
    nz, mask,
    occ_ref, ints_ref, metric_ref, virt_ref, out_ref,
    gat, metric2, select, wide, yout, yin, x4p, x4, xt, bf, tq, rb, aq, den, part, pout, pin, vcol,
    m_s, m_r, y_s, y_r, es, er, os_, or_, bs, br, xs, xr, rs, rr, cs, cr, ps, pr,
):
    aux = lax.axis_index("aux")
    pair = lax.axis_index("pair")
    z = aux // 2
    yh = aux % 2
    rows, _, vir = ints_ref.shape
    up = lax.rem(z + 1, nz) * 2 + yh
    down = lax.rem(z + nz - 1, nz) * 2 + yh
    across = z * 2 + 1 - yh
    half = nz // 2
    far = nz // 2
    group = aux // 4
    q = aux % 4
    quarter = vir // 4
    used = quarter * 5 // 2
    span = tq.shape[1] // far
    mate = lambda k: group * 4 + lax.rem(q + k, 4)
    distant = lambda k: lax.rem(group + k, far) * 4 + q

    barrier = pltpu.get_barrier_semaphore()
    for other in [up, down] + [mate(k) for k in range(1, 4)] + [distant(k) for k in range(1, far)]:
        pl.semaphore_signal(barrier, inc=1, device_id={"aux": other, "pair": pair}, device_id_type=MESH)
    other_pair = flip(pair, mask)
    pl.semaphore_signal(barrier, inc=1, device_id={"aux": aux, "pair": other_pair}, device_id_type=MESH)
    pl.semaphore_wait(barrier, 5 + far)

    def remote(src, dst, s, r, dev_aux, dev_pair=None):
        return pltpu.make_async_remote_copy(
            src_ref=src, dst_ref=dst, send_sem=s, recv_sem=r,
            device_id={"aux": dev_aux, "pair": pair if dev_pair is None else dev_pair},
            device_id_type=MESH,
        )

    m_copy = remote(metric_ref, metric2, m_s, m_r, across)
    gat[z] = pack(ints_ref[:, 0, :])

    def relay(d, k):
        block = lax.rem(z - 2 * k + 2 * nz, nz) if d == 0 else lax.rem(z + 2 * k, nz)
        ref = gat.at[block]
        if k == half // 2 - 1:
            size = gat.shape[1] // 2
            ref = gat.at[block, pl.ds(d * size, size)]
        return remote(ref, ref, es.at[d, k], er.at[d, k], distant(1) if d == 0 else distant(far - 1))

    def side(d, k):
        block = lax.rem(z - 2 * k + 2 * nz, nz) if d == 0 else lax.rem(z + 2 * k, nz)
        ref = gat.at[block]
        return remote(ref, ref, os_.at[d, k], or_.at[d, k], up if d == 0 else down)

    steps = half // 2
    for d in range(2):
        relay(d, 0).start()
    for d in range(2):
        side(d, 0).start()
    m_copy.start()

    def choose_columns(ref, base):
        def one(b, carry):
            both = ref[:, pl.ds(pl.multiple_of(b * 2 * rows, 2 * rows), 2 * rows)]
            select[b, base:base + rows] = jnp.where(yh == 0, both[:, :rows], both[:, rows:])
            return carry

        lax.fori_loop(0, nz, one, 0)

    choose_columns(metric_ref, 0)
    wide[...] = jnp.zeros_like(wide)
    tq[...] = jnp.zeros_like(tq)
    den[...] = jnp.full(den.shape, -1.0, jnp.float32)
    v_row = virt_ref[...].reshape(1, vir)
    vcol[...] = jnp.broadcast_to(v_row, (8, vir)).T
    own_rows = vcol[pl.ds(pl.multiple_of(q * quarter, 8), quarter), :1]
    short = quarter // 2
    for which in range(2):
        own = occ_ref[pair]
        e = own + own if which == 0 else own + occ_ref[other_pair]
        den[which, :used] = pack(e - own_rows - v_row)

    for k in range(1, steps):
        for d in range(2):
            relay(d, k - 1).wait_recv()
            relay(d, k).start()
        for d in range(2):
            side(d, k).start()

    def accumulate(block):
        wide[...] += dot(select[block], unpack(gat[block]), ((1,), (0,)))

    m_copy.wait_recv()
    choose_columns(metric2, rows)

    def near(i, carry):
        accumulate(lax.rem(z + i, nz))
        return carry

    for d in range(2):
        for k in range(steps - 1):
            side(d, k).wait_recv()
    lax.fori_loop(half + 2, 2 * nz - half - 1, near, 0)
    for d in range(2):
        side(d, steps - 1).wait_recv()
    for d in range(2):
        relay(d, steps - 1).wait_recv()
    lax.fori_loop(half - 1, half + 2, near, 0)
    yout[...] = pack(wide[rows:])
    y_copy = remote(yout, yin, y_s, y_r, across)
    y_copy.start()
    y_copy.wait_recv()
    bf[0] = pack(wide[:rows]) + yin[...]

    b_copy = remote(bf.at[0], bf.at[1], bs, br, aux, other_pair)
    b_copy.start()

    def swap(h, k):
        return remote(bf.at[h], x4p.at[h, q], xs.at[h, k - 1], xr.at[h, k - 1], mate(k))

    for k in range(1, 4):
        swap(0, k).start()
    x4p[0, q] = bf[0]

    def put(h, value):
        tq[h, :used] = pack(value)

    def piece(u):
        return pl.ds(pl.multiple_of(u * span, 8), span)

    def scatter(h, k):
        to = lax.rem(group + k, far)
        return remote(tq.at[h, piece(to)], rb.at[h, k - 1], rs.at[h, k - 1], rr.at[h, k - 1], distant(k))

    def reduce(h):
        value = tq[h, piece(group)]
        for k in range(1, far):
            scatter(h, k).wait_recv()
            value = value + rb[h, k - 1]
        aq[h, piece(group)] = value / den[h, piece(group)]

    def spread(h, k):
        ref = aq.at[h, piece(group)]
        return remote(ref, ref, cs.at[h, k - 1], cr.at[h, k - 1], distant(k))

    b_copy.wait_recv()
    for k in range(1, 4):
        swap(1, k).start()
    x4p[1, q] = bf[1]
    own_quarter = pl.ds(pl.multiple_of(q * quarter, 8), quarter)

    def sums(h, carry):
        for k in range(1, 4):
            swap(h, k).wait_recv()
        for src in range(4):
            x4[h, src * rows:(src + 1) * rows] = unpack(x4p[h, src])
        xt[h] = x4[h].T
        put(h, dot(xt[h, own_quarter], x4[0], ((1,), (0,))))
        for k in order:
            scatter(h, k).start()
        return carry

    def spreads(h, carry):
        reduce(h)
        for k in order:
            spread(h, k).start()
        return carry

    def densities(h, carry):
        def arrive(k, inner):
            spread(h, k).wait_recv()
            return inner

        lax.fori_loop(1, far, arrive, 0)
        weight = (h + 1).astype(jnp.float32)
        part[...] += dot(weight * xt[h, own_quarter], unpack(aq[h, :used]), ((0,), (0,)))
        return carry

    order = [k for near_k in range(far // 2, 0, -1) for k in (near_k, far - near_k)][1:]
    part[...] = jnp.zeros_like(part)
    lax.fori_loop(0, 2, sums, 0)
    lax.fori_loop(0, 2, spreads, 0)
    lax.fori_loop(0, 2, densities, 0)
    swapped = dot(x4[1], unpack(aq[1, :used]), ((1,), (1,)))
    for g in range(4):
        @pl.when(q == g)
        def _():
            part[:, g * quarter:(g + 1) * quarter] -= swapped

    def give(k):
        return remote(pout.at[k - 1], pin.at[k - 1], ps.at[k - 1], pr.at[k - 1], mate(k))

    def block(k):
        return pack(part[pl.ds(pl.multiple_of(lax.rem(q + k, 4) * rows, 8), rows)])

    def start(k, carry):
        pout[k - 1] = block(k)
        give(k).start()
        return carry

    def finish(k, total):
        give(k).wait_recv()
        return total + pin[k - 1]

    lax.fori_loop(1, 4, start, 0)
    out_ref[:, 0, :] = unpack(lax.fori_loop(1, 4, finish, block(0)))

    for d in range(2):
        for k in range(steps):
            relay(d, k).wait_send()
            side(d, k).wait_send()
    for copy in (m_copy, y_copy, b_copy):
        copy.wait_send()

    def drain_mates(k, carry):
        for h in range(2):
            swap(h, k).wait_send()
        give(k).wait_send()
        return carry

    def drain_far(k, carry):
        for h in range(2):
            scatter(h, k).wait_send()
            spread(h, k).wait_send()
        return carry

    lax.fori_loop(1, 4, drain_mates, 0)
    lax.fori_loop(1, far, drain_far, 0)


def window(nz, mask, integrals, metric_root, occ_energy, virt_energy):
    rows, _, vir = integrals.shape
    half = nz // 2
    far = nz // 2
    quarter = vir // 4
    packed = rows * 5 // 2
    padded = -(-(quarter * 5 // 2) // (8 * far)) * 8 * far
    vm = pl.BlockSpec(memory_space=pltpu.VMEM)
    sm = pl.BlockSpec(memory_space=pltpu.SMEM)
    f32 = jnp.float32
    dma = pltpu.SemaphoreType.DMA
    out = pl.pallas_call(
        functools.partial(kernel, nz, mask),
        out_shape=jax.ShapeDtypeStruct((rows, 1, vir), f32),
        in_specs=[sm, vm, vm, vm],
        out_specs=vm,
        scratch_shapes=[
            pltpu.VMEM((nz, packed, 128), f32),
            pltpu.VMEM(metric_root.shape, f32),
            pltpu.VMEM((nz, 2 * rows, rows), f32),
            pltpu.VMEM((2 * rows, vir), f32),
            pltpu.VMEM((packed, 128), f32),
            pltpu.VMEM((packed, 128), f32),
            pltpu.VMEM((2, 4, packed, 128), f32),
            pltpu.VMEM((2, 4 * rows, vir), f32),
            pltpu.VMEM((2, vir, 4 * rows), f32),
            pltpu.VMEM((2, packed, 128), f32),
            pltpu.VMEM((2, padded, 128), f32),
            pltpu.VMEM((2, far - 1, padded // far, 128), f32),
            pltpu.VMEM((2, padded, 128), f32),
            pltpu.VMEM((2, padded, 128), f32),
            pltpu.VMEM((4 * rows, vir), f32),
            pltpu.VMEM((3, packed, 128), f32),
            pltpu.VMEM((3, packed, 128), f32),
            pltpu.VMEM((vir, 8), f32),
            dma, dma,
            dma, dma,
            dma((2, half // 2)), dma((2, half // 2)),
            dma((2, half // 2)), dma((2, half // 2)),
            dma, dma,
            dma((2, 3)), dma((2, 3)),
            dma((2, far - 1)), dma((2, far - 1)),
            dma((2, far - 1)), dma((2, far - 1)),
            dma((3,)), dma((3,)),
        ],
        compiler_params=pltpu.CompilerParams(collective_id=mask, has_side_effects=True),
    )(
        occ_energy, integrals, metric_root, virt_energy,
    )
    return out


def shards(nz, integrals, metric_root, occ_energy, virt_energy, partner):
    count = lax.axis_size("pair")
    branches = [functools.partial(window, nz, mask) for mask in range(1, count)]
    return lax.switch(partner[0, 0] - 1, branches, integrals, metric_root, occ_energy, virt_energy)


def solution(mesh):
    nz = mesh.shape["aux"] // 2
    in_specs = (P("aux", "pair", None), P("aux", None), P(), P(), P())
    return jax.shard_map(
        functools.partial(shards, nz), mesh=mesh, in_specs=in_specs,
        out_specs=P("aux", "pair", None), check_vma=False,
    )
```

time: 97 us -> 91.1 us (0.939)
  the two profiles are of different devices: /device:TPU:6 before, /device:TPU:14 now
where the time goes in v5:
time: 91.1 us; the launch traced here: 89.4 us
  Pallas kernels  86.9 us (95%)
  local copies, waits for them, and re-layouts  1.96 us (2%)
    pallas_call x1, Pallas kernels, window(): pl.pallas_call(functools.partial(kernel, nz, mask), out_shape=jax.ShapeDt...  86.9 us
    unnamed x7, local copies, waits for them, and re-layouts  1.96 us

profile of v5, /device:TPU:14, one launch (start us, length us, event | category | flops | bytes accessed | tf_op | source)
XLA Modules:
  0.0 89.4 jit_solution(13168449023075202174)
XLA Ops:
  0.0 0.0 copy-start.2
  0.0 0.7 copy-done.2
  0.7 0.0 copy-start
  0.7 0.0 copy-start.1
  0.7 0.7 copy-done
  1.4 0.0 copy-done.1
  1.4 87.4 %conditional.1 = (f32[64,1,320]{2,1,0:T(1,128)S(1)}) conditional(s32[]{:T(128)} %bitcast, (f32[16]{0:T(128)S(1)}, f32[64,1,320]{2,1,0:T(1,128)}, f32[64,2048]{1,0:T(8,128)}, f32[320]{0:T(512)S(1)}) %tuple.96, (f32[16]{0:T(128)S(1)}, f32[64,1,320]{2,1,0:T(1,128)}, f32[64,2048]{1,0:T(8,128)}, ...), branch_computations={%region_0.0_spmd, %region_1.0_spmd, %region_2.0_spmd, %region_3.0_... | conditional | bytes 8 | solution.py:330
  1.4 86.9 %branch_0_fun.1 = f32[64,1,320]{2,1,0:T(1,128)S(1)} custom-call(f32[16]{0:T(128)S(1)} %get-tuple-element.124.occ_ref, f32[64,1,320]{2,1,0:T(1,128)} %get-tuple-element.130.ints_ref, f32[64,2048]{1,0:T(8,128)} %get-tuple-element.131.metric_ref, f32[320]{0:T(512)S(1)} %get-tuple-element.132.virt_ref), custom_call_target="tpu_custom_call" | custom-call | tf_op jit(solution)/shard_map/cond/branch_0_fun/pallas_call | solution.py:286
  88.8 0.6 copy.37
Async XLA Ops:
  0.0 0.7 copy-start.2
  0.7 0.7 copy-start
  0.7 0.7 copy-start.1

commit v6 on v5

v6 whole, which is shorter than its diff:
```python
import functools

import jax
import jax.numpy as jnp
from jax import lax
from jax.experimental import pallas as pl
from jax.experimental.pallas import tpu as pltpu
from jax.sharding import PartitionSpec as P

MESH = pl.DeviceIdType.MESH

def flip(index, mask):
    for bit in (1, 2, 4, 8):
        if mask & bit:
            index = index + bit - 2 * bit * ((index // bit) % 2)
    return index


def split(value):
    high = value.astype(jnp.bfloat16)
    return high, (value - high.astype(jnp.float32)).astype(jnp.bfloat16)


def dot(left, right, dims):
    l_high, l_low = split(left)
    r_high, r_low = split(right)
    one = functools.partial(
        lax.dot_general, dimension_numbers=(dims, ((), ())), preferred_element_type=jnp.float32
    )
    return one(l_high, r_high) + (one(l_high, r_low) + one(l_low, r_high))


def pack(value):
    short = value.shape[0] // 2
    tail = jnp.concatenate([value[:short, 256:], value[short:, 256:]], axis=1)
    return jnp.concatenate([value[:, :128], value[:, 128:256], tail], axis=0)


def unpack(value):
    rows = value.shape[0] * 2 // 5
    tail = jnp.concatenate([value[2 * rows:, :64], value[2 * rows:, 64:]], axis=0)
    return jnp.concatenate([value[:rows], value[rows:2 * rows], tail], axis=1)


def kernel(
    nz, mask,
    occ_ref, ints_ref, metric_ref, virt_ref, out_ref,
    tri, tri_rb, tri_aq, tri_den,
    gat, cols, wide, yout, yin, x4p, x4, xt, bf, tq, rb, aq, den, part, part_t, pout, pin, vcol,
    m_s, m_r, h_s, h_r, y_s, y_r, es, er, bs, br, xs, xr, rs, rr, cs, cr, ps, pr,
):
    aux = lax.axis_index("aux")
    pair = lax.axis_index("pair")
    rows, _, vir = ints_ref.shape
    far = nz // 2
    group = aux // 4
    q = aux % 4
    quarter = vir // 4
    used = quarter * 5 // 2
    span = tq.shape[0] // far
    tri_span = tri.shape[0] // far
    side_of = tri.shape[0] // 2

    is0, is1 = (3 - q) // 3, (q % 2) * (1 - q // 2)
    is2, is3 = (q // 2) * (1 - q % 2), q // 3

    def place(i, j):
        corner = is0 * i * (1 - j)
        row = i + 2 * is2 + 2 * j * is3 + 3 * corner
        column = j * (1 - is3) + 2 * (is1 + is2) + 4 * is3 + 4 * corner
        mirrored = is1 + is3 + is0 * (1 - i) * j
        at = lambda n: pl.ds(pl.multiple_of(n * side_of, 8), side_of)
        return at(row), at(column), mirrored
    mate = lambda k: group * 4 + lax.rem(q + k, 4)
    distant = lambda k: lax.rem(group + k, far) * 4 + q

    barrier = pltpu.get_barrier_semaphore()
    def hello(dev_aux, dev_pair):
        pl.semaphore_signal(barrier, inc=1, device_id={"aux": dev_aux, "pair": dev_pair}, device_id_type=MESH)

    def greet(k, carry):
        hello(distant(k), pair)
        return carry

    core = pair % 2
    twin = flip(pair, 1)
    hello(aux, twin)
    for k in range(1, 4):
        hello(mate(k), pair)
    lax.fori_loop(1, far, greet, 0)
    other_pair = flip(pair, mask)
    hello(aux, other_pair)
    pl.semaphore_wait(barrier, 4 + far)

    def remote(src, dst, s, r, dev_aux, dev_pair=None):
        return pltpu.make_async_remote_copy(
            src_ref=src, dst_ref=dst, send_sem=s, recv_sem=r,
            device_id={"aux": dev_aux, "pair": pair if dev_pair is None else dev_pair},
            device_id_type=MESH,
        )

    steps = far // 2
    gat[group] = pack(ints_ref[:, 0, :])

    def relay(d, k):
        ref = gat.at[lax.rem(group - k + far, far) if d == 0 else lax.rem(group + k, far)]
        if k == steps - 1:
            size = gat.shape[1] // 2
            ref = ref.at[pl.ds(d * size, size)]
        return remote(ref, ref, es.at[d, k], er.at[d, k], distant(1) if d == 0 else distant(far - 1))

    for d in range(2):
        relay(d, 0).start()

    pairs = cols.shape[2]

    def choose_columns(n, carry):
        k, v = n // pairs, n % pairs
        their = lax.rem(q + k, 4)
        halves = []
        for h in range(2):
            tile = (2 * v + h) * 2 + their // 2
            both = metric_ref[:, pl.ds(pl.multiple_of(tile * 2 * rows, 2 * rows), 2 * rows)]
            halves.append(jnp.where(their % 2 == 0, both[:, :rows], both[:, rows:]))
        cols[0, k, v] = jnp.concatenate(halves, axis=1)
        return carry

    lax.fori_loop(0, 4 * pairs, choose_columns, 0)

    def bring(k, c):
        v = core * (pairs // 2) + c
        return remote(cols.at[0, k, v], cols.at[1, k, v], m_s.at[k - 1, c], m_r.at[k - 1, c], mate(k))

    def pass_on(k, c):
        ref = cols.at[1, k, core * (pairs // 2) + c]
        return remote(ref, ref, h_s.at[k - 1, c], h_r.at[k - 1, c], aux, twin)

    def mates_do(act):
        def one(k, carry):
            act(k)
            return carry

        lax.fori_loop(1, 4, one, 0)

    def brings(c):
        mates_do(lambda k: bring(k, c).start())

    def passes(c):
        def one(k):
            bring(k, c).wait_recv()
            pass_on(k, c).start()

        mates_do(one)

    brings(0)
    cols[1, 0] = cols[0, 0]
    wide[...] = jnp.zeros_like(wide)
    tq[...] = jnp.zeros_like(tq)
    den[...] = jnp.full(den.shape, -1.0, jnp.float32)
    v_row = virt_ref[...].reshape(1, vir)
    vcol[...] = jnp.broadcast_to(v_row, (8, vir)).T
    own_rows = vcol[pl.ds(pl.multiple_of(q * quarter, 8), quarter), :1]
    own = occ_ref[pair]
    den[:used] = pack(own + occ_ref[other_pair] - own_rows - v_row)

    def tri_dens(i, carry):
        subs = []
        for j in range(2):
            row, column, _ = place(i, j)
            subs.append(own + own - vcol[row, :1] - vcol[column].T[:1])
        tri_den[pl.ds(pl.multiple_of(i * side_of, 8), side_of)] = jnp.concatenate(subs, axis=1)
        return carry

    lax.fori_loop(0, 2, tri_dens, 0)

    for k in range(1, steps):
        for d in range(2):
            relay(d, k - 1).wait_recv()
            relay(d, k).start()
        if k <= pairs // 2:
            passes(k - 1)
        if k < pairs // 2:
            brings(k)
    for c in range(pairs // 2):
        mates_do(lambda k: pass_on(k, c).wait_recv())

    def accumulate(i, carry):
        block = lax.rem(group + i, far)
        both = cols[1, :, block // 2].reshape(4 * rows, 2 * rows)
        chosen = jnp.where(block % 2 == 0, both[:, :rows], both[:, rows:])
        wide[...] += dot(chosen, unpack(gat[block]), ((1,), (0,)))
        return carry

    def in_turn(n, carry):
        @pl.when(n == far - 1)
        def _():
            for d in range(2):
                relay(d, steps - 1).wait_recv()
        return accumulate(steps + 1 + n, carry)

    lax.fori_loop(0, far, in_turn, 0)

    def give_back(k):
        return remote(yout.at[k - 1], yin.at[k - 1], y_s.at[k - 1], y_r.at[k - 1], mate(4 - k))

    def start_back(k, carry):
        yout[k - 1] = pack(wide[pl.ds(pl.multiple_of(k * rows, 8), rows)])
        give_back(k).start()
        return carry

    def finish_back(k, total):
        give_back(k).wait_recv()
        return total + yin[k - 1]

    lax.fori_loop(1, 4, start_back, 0)
    bf[0] = lax.fori_loop(1, 4, finish_back, pack(wide[:rows]))

    b_copy = remote(bf.at[0], bf.at[1], bs, br, aux, other_pair)
    b_copy.start()

    def swap(h, k):
        return remote(bf.at[h], x4p.at[h, q], xs.at[h, k - 1], xr.at[h, k - 1], mate(k))

    mates_do(lambda k: swap(0, k).start())
    x4p[0, q] = bf[0]

    streams = ((tri, tri_rb, tri_aq, tri_den, tri_span), (tq, rb, aq, den, span))

    def piece(h, u):
        size = streams[h][4]
        return pl.ds(pl.multiple_of(u * size, 8), size)

    def scatter(h, k):
        ref = streams[h][0].at[piece(h, lax.rem(group + k, far))]
        return remote(ref, streams[h][1].at[k - 1], rs.at[h, k - 1], rr.at[h, k - 1], distant(k))

    def spread(h, k):
        ref = streams[h][2].at[piece(h, group)]
        return remote(ref, ref, cs.at[h, k - 1], cr.at[h, k - 1], distant(k))

    def send(copy, h):
        def one(n, carry):
            k = far // 2 + (n // 2) * (2 * (n % 2) - 1)
            copy(h, k).start()
            return carry

        lax.fori_loop(1, far, one, 0)

    def reduce(h):
        def add(k, value):
            scatter(h, k).wait_recv()
            return value + streams[h][1][k - 1]

        mine = piece(h, group)
        streams[h][2][mine] = lax.fori_loop(1, far, add, streams[h][0][mine]) / streams[h][3][mine]

    b_copy.wait_recv()
    mates_do(lambda k: swap(1, k).start())
    x4p[1, q] = bf[1]
    own_quarter = pl.ds(pl.multiple_of(q * quarter, 8), quarter)

    def sums(h, carry):
        mates_do(lambda k: swap(h, k).wait_recv())

        def open_up(src, inner):
            x4[h, pl.ds(pl.multiple_of(src * rows, 8), rows)] = unpack(x4p[h, src])
            return inner

        lax.fori_loop(0, 4, open_up, 0)
        xt[h] = x4[h].T

        @pl.when(h == 0)
        def _():
            def blocks(i, inner):
                subs = []
                for j in range(2):
                    row, column, _ = place(i, j)
                    subs.append(dot(xt[0, row], xt[0, column], ((1,), (1,))))
                tri[pl.ds(pl.multiple_of(i * side_of, 8), side_of)] = jnp.concatenate(subs, axis=1)
                return inner

            lax.fori_loop(0, 2, blocks, 0)
            send(scatter, 0)

        @pl.when(h == 1)
        def _():
            tq[:used] = pack(dot(xt[1, own_quarter], x4[0], ((1,), (0,))))
            send(scatter, 1)
        return carry

    def spread_all(h):
        def arrive(k, inner):
            spread(h, k).wait_recv()
            return inner

        lax.fori_loop(1, far, arrive, 0)

    def tri_densities(i, carry):
        for j in range(2):
            row, column, mirrored = place(i, j)
            block = tri_aq[pl.ds(pl.multiple_of(i * side_of, 8), side_of)][:, j * side_of:(j + 1) * side_of]
            part_t[column] += dot(block, xt[0, row], ((0,), (0,)))
            part_t[row] += mirrored.astype(jnp.float32) * dot(block, xt[0, column], ((1,), (0,)))
        return carry

    part_t[...] = jnp.zeros_like(part_t)
    lax.fori_loop(0, 2, sums, 0)
    for h in range(2):
        reduce(h)
        send(spread, h)
    spread_all(0)
    lax.fori_loop(0, 2, tri_densities, 0)
    spread_all(1)
    cross = unpack(aq[:used])
    part_t[...] += dot(cross, 2.0 * xt[1, own_quarter], ((0,), (0,)))
    part_t[own_quarter] -= dot(cross, xt[1], ((1,), (0,)))
    part[...] = part_t[...].T

    def give(k):
        return remote(pout.at[k - 1], pin.at[k - 1], ps.at[k - 1], pr.at[k - 1], mate(k))

    def rows_of(k):
        return pack(part[pl.ds(pl.multiple_of(lax.rem(q + k, 4) * rows, 8), rows)])

    def start(k, carry):
        pout[k - 1] = rows_of(k)
        give(k).start()
        return carry

    def finish(k, total):
        give(k).wait_recv()
        return total + pin[k - 1]

    lax.fori_loop(1, 4, start, 0)
    out_ref[:, 0, :] = unpack(lax.fori_loop(1, 4, finish, rows_of(0)))

    for d in range(2):
        for k in range(steps):
            relay(d, k).wait_send()
    b_copy.wait_send()

    def drain_mates(k, carry):
        for h in range(2):
            swap(h, k).wait_send()
        give(k).wait_send()
        give_back(k).wait_send()
        for c in range(pairs // 2):
            bring(k, c).wait_send()
            pass_on(k, c).wait_send()
        return carry

    def drain_far(k, carry):
        for h in range(2):
            scatter(h, k).wait_send()
            spread(h, k).wait_send()
        return carry

    lax.fori_loop(1, 4, drain_mates, 0)
    lax.fori_loop(1, far, drain_far, 0)


def window(nz, mask, integrals, metric_root, occ_energy, virt_energy):
    rows, _, vir = integrals.shape
    half = nz // 2
    far = nz // 2
    quarter = vir // 4
    packed = rows * 5 // 2
    padded = -(-(quarter * 5 // 2) // (8 * far)) * 8 * far
    vm = pl.BlockSpec(memory_space=pltpu.VMEM)
    sm = pl.BlockSpec(memory_space=pltpu.SMEM)
    f32 = jnp.float32
    dma = pltpu.SemaphoreType.DMA
    out = pl.pallas_call(
        functools.partial(kernel, nz, mask),
        out_shape=jax.ShapeDtypeStruct((rows, 1, vir), f32),
        in_specs=[sm, vm, vm, vm],
        out_specs=vm,
        scratch_shapes=[
            pltpu.VMEM((2 * rows, 128), f32),
            pltpu.VMEM((far - 1, 2 * rows // far, 128), f32),
            pltpu.VMEM((2 * rows, 128), f32),
            pltpu.VMEM((2 * rows, 128), f32),
            pltpu.VMEM((far, packed, 128), f32),
            pltpu.VMEM((2, 4, far // 2, rows, 2 * rows), f32),
            pltpu.VMEM((4 * rows, vir), f32),
            pltpu.VMEM((3, packed, 128), f32),
            pltpu.VMEM((3, packed, 128), f32),
            pltpu.VMEM((2, 4, packed, 128), f32),
            pltpu.VMEM((2, 4 * rows, vir), f32),
            pltpu.VMEM((2, vir, 4 * rows), f32),
            pltpu.VMEM((2, packed, 128), f32),
            pltpu.VMEM((padded, 128), f32),
            pltpu.VMEM((far - 1, padded // far, 128), f32),
            pltpu.VMEM((padded, 128), f32),
            pltpu.VMEM((padded, 128), f32),
            pltpu.VMEM((4 * rows, vir), f32),
            pltpu.VMEM((vir, 4 * rows), f32),
            pltpu.VMEM((3, packed, 128), f32),
            pltpu.VMEM((3, packed, 128), f32),
            pltpu.VMEM((vir, 8), f32),
            dma((3, far // 4)), dma((3, far // 4)),
            dma((3, far // 4)), dma((3, far // 4)),
            dma((3,)), dma((3,)),
            dma((2, far // 2)), dma((2, far // 2)),
            dma, dma,
            dma((2, 3)), dma((2, 3)),
            dma((2, far - 1)), dma((2, far - 1)),
            dma((2, far - 1)), dma((2, far - 1)),
            dma((3,)), dma((3,)),
        ],
        compiler_params=pltpu.CompilerParams(collective_id=mask, has_side_effects=True),
    )(
        occ_energy, integrals, metric_root, virt_energy,
    )
    return out


def shards(nz, integrals, metric_root, occ_energy, virt_energy, partner):
    count = lax.axis_size("pair")
    branches = [functools.partial(window, nz, mask) for mask in range(1, count)]
    return lax.switch(partner[0, 0] - 1, branches, integrals, metric_root, occ_energy, virt_energy)


def solution(mesh):
    nz = mesh.shape["aux"] // 2
    in_specs = (P("aux", "pair", None), P("aux", None), P(), P(), P())
    return jax.shard_map(
        functools.partial(shards, nz), mesh=mesh, in_specs=in_specs,
        out_specs=P("aux", "pair", None), check_vma=False,
    )
```

time: 91.1 us -> 88.3 us (0.969)
  the two profiles are of different devices: /device:TPU:14 before, /device:TPU:6 now
where the time goes in v6:
time: 88.3 us; the launch traced here: 87.1 us
  Pallas kernels  84.4 us (96%)
  local copies, waits for them, and re-layouts  1.96 us (2%)
    pallas_call x1, Pallas kernels, window(): pl.pallas_call(functools.partial(kernel, nz, mask), out_shape=jax.ShapeDt...  84.4 us
    unnamed x7, local copies, waits for them, and re-layouts  1.96 us

profile of v6, /device:TPU:6, one launch (start us, length us, event | category | flops | bytes accessed | tf_op | source)
XLA Modules:
  0.0 87.1 jit_solution(16301372767682466815)
XLA Ops:
  0.0 0.0 copy-start.2
  0.0 0.7 copy-done.2
  0.7 0.0 copy-start
  0.7 0.0 copy-start.1
  0.7 0.7 copy-done
  1.4 0.0 copy-done.1
  1.4 85.0 %conditional.1 = (f32[64,1,320]{2,1,0:T(1,128)S(1)}) conditional(s32[]{:T(128)} %bitcast, (f32[16]{0:T(128)S(1)}, f32[64,1,320]{2,1,0:T(1,128)}, f32[64,2048]{1,0:T(8,128)}, f32[320]{0:T(512)S(1)}) %tuple.96, (f32[16]{0:T(128)S(1)}, f32[64,1,320]{2,1,0:T(1,128)}, f32[64,2048]{1,0:T(8,128)}, ...), branch_computations={%region_0.0_spmd, %region_1.0_spmd, %region_2.0_spmd, %region_3.0_... | conditional | bytes 8 | solution.py:421
  1.4 84.4 %branch_11_fun.1 = f32[64,1,320]{2,1,0:T(1,128)S(1)} custom-call(f32[16]{0:T(128)S(1)} %get-tuple-element.185.occ_ref, f32[64,1,320]{2,1,0:T(1,128)} %get-tuple-element.186.ints_ref, f32[64,2048]{1,0:T(8,128)} %get-tuple-element.187.metric_ref, f32[320]{0:T(512)S(1)} %get-tuple-element.188.virt_ref), custom_call_target="tpu_custom_call" | custom-call | tf_op jit(solution)/shard_map/cond/branch_11_fun/pallas_call | solution.py:373
  86.4 0.6 copy.37
Async XLA Ops:
  0.0 0.7 copy-start.2
  0.7 0.7 copy-start
  0.7 0.7 copy-start.1
